TPU v7x, 32 devices: a whole 2x2x4 slice. The times are simulated.
32 devices in a mesh: row: 4 (over x, core), col: 8 (over z, y).
Axes of the slice: x: 2, y: 2, z: 4, core: 2. Of those that a mesh axis runs over, the one named last changes fastest.
Arguments:
- design: bfloat16 [18432, 2048], P(('row', 'col')), may hold values from -0.19921875 to 0.19921875
- arc_filter: bfloat16 [2048, 2048], replicated, may hold values from -0.59765625 to 0.59765625
- arc_of_row: int32 [2048], replicated, may hold values from 0 to 255, never falling along the last dimension, each value on 1 to 512 neighbouring positions
- terr_stored: bfloat16 [18432, 128], P(('row', 'col')), may hold values from -3 to 3
- block_order: int32 [144], P('row'), may hold values from 0 to 143, as said below
- directions: float32 [18432, 256], P(('row', 'col')), may hold values from -6 to 6
Outputs:
- normals: float32 [4, 8, 576, 18432], P(None, 'col', None, 'row')
- products: float32 [18432, 256], P(('row', 'col'))
Inputs may be any that keep to these rules, and one draw needn't show every extreme that they name: `arc_of_row`: arc numbers never fall along the observations. `block_order`: each aligned group of 36 consecutive entries (the blocks of one block of 4608 unknowns) is a permutation of the positions of that same group.
All inputs are finite; a program needn't handle non-finite values.
Results may differ from a plain program's by a relative error of at most 0.00045.
Values may be sent and summed in bfloat16 or wider, within the bound.
A program may use at most 192 MiB of HBM per device.

v0:
```python
import jax
import jax.numpy as jnp
from jax import lax
from jax.sharding import PartitionSpec as P


def whiten(design, arc_filter, arc_of_row):
    positions = jnp.arange(arc_filter.shape[0], dtype=jnp.int32)
    keep_mask = (positions[:, None] > positions[None, :]) & (
        arc_of_row[:, None] == arc_of_row[None, :]
    )
    lower_part = jnp.where(keep_mask, arc_filter, jnp.zeros_like(arc_filter))
    mixed_part = lax.dot_general(
        design, lower_part, (((1,), (1,)), ((), ())), preferred_element_type=jnp.float32
    )
    return (design.astype(jnp.float32) + mixed_part).astype(jnp.bfloat16)


def body(design, arc_filter, arc_of_row, terr_stored, block_order, directions):
    whitened = whiten(design, arc_filter, arc_of_row)
    own_width = whitened.shape[0]
    rows_block, terr_rows = (
        lax.all_gather(whitened, "col", axis=0, tiled=True),
        lax.all_gather(terr_stored, "col", axis=0, tiled=True),
    )
    cols_block = lax.all_gather(whitened, "row", axis=0, tiled=True)
    normal_tile = lax.dot_general(
        cols_block, rows_block, (((1,), (1,)), ((), ())), preferred_element_type=jnp.float32
    )
    block_size = terr_rows.shape[1]
    span_rows = terr_rows.shape[0]
    group_count = span_rows // block_size
    row_index = lax.axis_index("row")
    col_index = lax.axis_index("col")
    local_order = block_order - row_index * group_count
    selector = (local_order[None, :] == jnp.arange(group_count, dtype=jnp.int32)[:, None]).astype(
        jnp.float32
    )
    stored = terr_rows.astype(jnp.float32).reshape(group_count, block_size, block_size)
    symmetric = jnp.triu(stored) + jnp.swapaxes(jnp.triu(stored, 1), 1, 2)
    ordered = jnp.einsum(
        "qt,tab->qab", selector, symmetric, precision=lax.Precision.HIGHEST
    ).reshape(span_rows, block_size)
    own_rows = lax.dynamic_slice_in_dim(ordered, col_index * own_width, own_width, 0)
    positions = col_index * own_width + jnp.arange(own_width, dtype=jnp.int32)
    onehot = (
        (positions // block_size)[:, None] == jnp.arange(group_count, dtype=jnp.int32)[None, :]
    ).astype(jnp.float32)
    terr_added = (onehot[:, :, None] * own_rows[:, None, :]).reshape(own_width, span_rows)
    current = lax.dynamic_slice_in_dim(normal_tile, row_index * own_width, own_width, 0)
    normal_tile = lax.dynamic_update_slice_in_dim(
        normal_tile, current + terr_added, row_index * own_width, 0
    )
    tile_rows = normal_tile.shape[0]
    partial_sum = jnp.dot(
        normal_tile,
        lax.all_gather(directions, "col", axis=0, tiled=True),
        precision=lax.Precision.HIGHEST,
        preferred_element_type=jnp.float32,
    )
    products = lax.psum_scatter(partial_sum, "row", scatter_dimension=0, tiled=True)
    normals = normal_tile.reshape(tile_rows // own_width, 1, own_width, span_rows)
    return (normals, products)


def solution(mesh):
    return jax.shard_map(
        body,
        mesh=mesh,
        in_specs=(
            P(("row", "col"), None),
            P(),
            P(),
            P(("row", "col"), None),
            P("row"),
            P(("row", "col"), None),
        ),
        out_specs=(P(None, "col", None, "row"), P(("row", "col"), None)),
        check_vma=False,
    )
```

profile of v0, /device:TPU:0, one launch (start us, length us, event | category | flops | bytes accessed | tf_op | source)
XLA Modules:
  0.0 640.6 jit_solution(7251335784853604112)
XLA Ops:
  7.2 0.0 all-gather.9.cloned.1.call-start
  7.2 0.7 all-gather.9.cloned.1.call-update
  7.9 0.0 all-gather.5.cloned.1.call-start
  7.9 11.9 %fusion.7 = bf16[576,2048]{1,0:T(8,128)(2,1)} fusion(bf16[576,2048]{1,0:T(8,128)(2,1)} %param.6, bf16[2048,2048]{1,0:T(8,128)(2,1)} %param.7, s32[2048]{0:T(1024)} %param.8), kind=kOutput, calls=%fused_computation.10 | convolution fusion | flops 4852154368 | bytes 13115392 | tf_op jit(solution)/shard_map/dot_general | solution.py:13
  19.8 0.0 copy-start.1
  19.8 0.0 all-gather.5.cloned.1.call-update
  19.8 0.0 all-gather.7.cloned.1.call-start
  19.9 0.7 all-gather.7.cloned.1.call-update
  20.6 0.0 all-gather.11.cloned.1.call-start
  20.6 0.5 all-gather.11.cloned.1.call-update
  21.1 0.0 reduce-scatter.2.cloned.1.call-start
  21.3 0.1 fusion.15
  21.4 0.0 copy-done.1
  21.4 32.6 %all-gather.9.cloned.1.call-done = bf16[4608,128]{1,0:T(8,128)(2,1)} async-done(((bf16[576,128]{1,0:T(8,128)(2,1)}), bf16[4608,128]{1,0:T(8,128)(2,1)}) %all-gather.9.cloned.1.call-update) | async-done | bytes 1179664 | tf_op jit(solution)/shard_map/all_gather | solution.py:24
  54.0 1.9 copy.12
  56.0 1.8 broadcast_select_fusion
  57.8 3.4 copy.14
  61.2 3.8 fusion.11
  65.0 0.5 copy.15
  65.5 7.0 %broadcast_multiply_fusion = f32[576,36,128]{2,1,0:T(8,128)} fusion(f32[576,128]{1,0:T(8,128)S(1)} %constant_dynamic-slice_fusion, f32[576,36]{1,0:T(8,128)S(1)} %fusion.15), kind=kLoop, calls=%fused_computation.8 | loop fusion | flops 2654208 | bytes 10994688 | tf_op jit(solution)/shard_map/mul | solution.py:49
  72.5 46.0 %all-gather.5.cloned.1.call-done = bf16[2304,2048]{1,0:T(8,128)(2,1)} async-done(((bf16[576,2048]{1,0:T(8,128)(2,1)}), bf16[2304,2048]{1,0:T(8,128)(2,1)}) %all-gather.5.cloned.1.call-update) | async-done | bytes 9437200 | tf_op jit(solution)/shard_map/all_gather | solution.py:26
  118.5 364.0 %all-gather.7.cloned.1.call-done = bf16[4608,2048]{1,0:T(8,128)(2,1)} async-done(((bf16[576,2048]{1,0:T(8,128)(2,1)}), bf16[4608,2048]{1,0:T(8,128)(2,1)}) %all-gather.7.cloned.1.call-update) | async-done | bytes 18874384 | tf_op jit(solution)/shard_map/all_gather | solution.py:23
  482.5 0.0 copy-start
  482.5 53.3 %fusion.24 = f32[2304,4608]{1,0:T(8,128)} fusion(bf16[2304,2048]{1,0:T(8,128)(2,1)} %all-gather.5.cloned.1.call-done, bf16[4608,2048]{1,0:T(8,128)(2,1)} %all-gather.7.cloned.1.call-done), kind=kOutput, calls=%fused_computation.39 | convolution fusion | flops 43486543872 | bytes 70778880 | tf_op jit(solution)/shard_map/dot_general | solution.py:27
  535.8 0.0 copy-done
  535.8 10.3 %fusion.2 = f32[2304,4608]{1,0:T(8,128)} fusion(f32[2304,4608]{1,0:T(8,128)} %fusion.24, s32[]{:T(128)S(6)} %select_n.29, f32[72,8,36,128]{3,2,1,0:T(8,128)S(1)} %bitcast.27), kind=kLoop, calls=%fused_computation.4 | loop fusion | flops 2654208 | bytes 31850500 | tf_op jit(solution)/shard_map/dynamic_update_slice | solution.py:51
  546.1 17.8 %all-gather.11.cloned.1.call-done = f32[4608,256]{1,0:T(8,128)} async-done(((f32[576,256]{1,0:T(8,128)}), f32[4608,256]{1,0:T(8,128)}) %all-gather.11.cloned.1.call-update) | async-done | bytes 4718608 | tf_op jit(solution)/shard_map/all_gather | solution.py:57
  563.9 38.9 %fusion.25 = f32[2304,256]{1,0:T(8,128)} fusion(f32[2304,4608]{1,0:T(8,128)} %fusion.2, f32[4608,256]{1,0:T(8,128)} %all-gather.11.cloned.1.call-done), kind=kOutput, calls=%fused_computation.40 | convolution fusion | flops 32614907904 | bytes 49545216 | tf_op jit(solution)/shard_map/dot_general | solution.py:55
  602.7 0.0 reduce-scatter.2.cloned.1.call-update
  602.8 31.3 %reduce-scatter.2.cloned.1.call-done = f32[576,256]{1,0:T(8,128)} async-done(((f32[2304,256]{1,0:T(8,128)}), f32[576,256]{1,0:T(8,128)}) %reduce-scatter.2.cloned.1.call-update) | async-done | bytes 589840 | tf_op jit(solution)/shard_map/reduce_scatter | solution.py:61
  (6 shorter events, 0.1 us)
Async XLA Ops:
  7.2 46.9 %all-gather.9.cloned.1.call-start = ((), (), s32[]{:S(2)}) async-start(), calls=%async_computation.3 | async-start | bytes 1327104 | tf_op jit(solution)/shard_map/all_gather | solution.py:24
  7.9 110.6 %all-gather.5.cloned.1.call-start = ((), (), s32[]{:S(2)}) async-start(), calls=%async_computation.1 | async-start | bytes 11796480 | tf_op jit(solution)/shard_map/all_gather | solution.py:26
  19.8 1.6 copy-start.1
  19.8 462.7 %all-gather.7.cloned.1.call-start = ((), (), s32[]{:S(2)}) async-start(), calls=%async_computation.2 | async-start | bytes 21233664 | tf_op jit(solution)/shard_map/all_gather | solution.py:23
  20.6 543.3 %all-gather.11.cloned.1.call-start = ((), (), s32[]{:S(2)}) async-start(), calls=%async_computation.4 | async-start | bytes 5308416 | tf_op jit(solution)/shard_map/all_gather | solution.py:57
  21.1 613.0 %reduce-scatter.2.cloned.1.call-start = ((), (), s32[]{:S(2)}) async-start(), calls=%async_computation.5 | async-start | bytes 2949120 | tf_op jit(solution)/shard_map/reduce_scatter | solution.py:61
  482.5 53.3 %copy-start = (f32[576,36,128]{2,1,0:T(8,128)S(1)}, f32[576,36,128]{2,1,0:T(8,128)}, u32[]{:S(2)}) copy-start(f32[576,36,128]{2,1,0:T(8,128)} %broadcast_multiply_fusion) | copy-start | bytes 31850500
Sparse Core Ops, SparseCore 0:
  10.2 43.8 all-gather.8
  55.6 62.8 all-gather.4
  120.1 362.3 all-gather.6
  484.5 79.2 all-gather.10
  602.9 31.1 reduce-scatter.1
where the time goes:
time: 641 us
  waiting for transfers between devices  494 us (77%)
  matrix products  108 us (17%)
  other arithmetic  19.3 us (3%)
  between operations  13.9 us (2%)
    all_gather x1, waiting for transfers between devices, body(): lax.all_gather(whitened, 'col', axis=0, tiled=True)  364 us
    dot_general x1, matrix products, body(): lax.dot_general(cols_block, rows_block, (((1,), (1,)), ((), ())), preferr...  53.3 us
    all_gather x1, waiting for transfers between devices, body(): cols_block = lax.all_gather(whitened, 'row', axis=0, tiled=True)  46 us
    dot_general x1, matrix products, body(): jnp.dot(normal_tile, lax.all_gather(directions, 'col', axis=0, tiled=True...  38.9 us
    all_gather x1, waiting for transfers between devices, body(): lax.all_gather(terr_stored, 'col', axis=0, tiled=True)  32.6 us
    reduce_scatter x1, waiting for transfers between devices, body(): lax.psum_scatter(partial_sum, 'row', scatter_dimension=0, tiled=True)  31.3 us
    all_gather x1, waiting for transfers between devices, body(): lax.all_gather(directions, 'col', axis=0, tiled=True)  17.8 us
  transfers between devices with their start and end apart: 5, of which 5 were waited for; matrix products, arithmetic and copies ran while one was open for 15% of the time, Pallas kernels for 0%

commit v1 on v0

--- a/solution.py
+++ b/solution.py
@@ -23,7 +23,12 @@
         lax.all_gather(whitened, "col", axis=0, tiled=True),
         lax.all_gather(terr_stored, "col", axis=0, tiled=True),
     )
-    cols_block = lax.all_gather(whitened, "row", axis=0, tiled=True)
+    ring = [whitened]
+    for hop in range(3):
+        ring.append(lax.ppermute(ring[-1], "row", [(dev, (dev + 1) % 4) for dev in range(4)]))
+    cols_block = jnp.roll(
+        jnp.concatenate(ring[::-1], axis=0), (lax.axis_index("row") + 1) * ring[0].shape[0], axis=0
+    )
     normal_tile = lax.dot_general(
         cols_block, rows_block, (((1,), (1,)), ((), ())), preferred_element_type=jnp.float32
     )

time: 641 us -> 575 us (0.90)
  waiting for transfers between devices: 494 us -> 403 us
  local copies, waits for them, and re-layouts: 5.85 us -> 25.9 us
    all_gather x1, waiting for transfers between devices: 364 us -> 291 us  [body(): lax.all_gather(whitened, 'col', axis=0, tiled=True)]
    ppermute x0 -> x3, waiting for transfers between devices: none -> 67.3 us  [body(): lax.ppermute(ring[-1], 'row', [(dev, (dev + 1) % 4) for dev in range(4)])]
    all_gather x1 -> x0, waiting for transfers between devices: 46 us -> none  [body(): cols_block = lax.all_gather(whitened, 'row', axis=0, tiled=True)]
    all_gather x1, waiting for transfers between devices: 32.6 us -> 0.02 us  [body(): lax.all_gather(terr_stored, 'col', axis=0, tiled=True)]
    unnamed x4 -> x15, local copies, waits for them, and re-layouts: 0.01 us -> 18.4 us
  transfers between devices with their start and end apart: 5 -> 7, of which waited for: 5 -> 6; matrix products, arithmetic and copies ran while one was open for 15% -> 21% of each run, Pallas kernels for 0% -> 0%
where the time goes in v1:
time: 575 us
  waiting for transfers between devices  403 us (70%)
  matrix products  109 us (19%)
  local copies, waits for them, and re-layouts  25.9 us (5%)
  other arithmetic  22.4 us (4%)
  between operations  13.9 us (2%)
    all_gather x1, waiting for transfers between devices, body(): lax.all_gather(whitened, 'col', axis=0, tiled=True)  291 us
    ppermute x3, waiting for transfers between devices, body(): lax.ppermute(ring[-1], 'row', [(dev, (dev + 1) % 4) for dev in range(4)])  67.3 us
    dot_general x1, matrix products, body(): lax.dot_general(cols_block, rows_block, (((1,), (1,)), ((), ())), preferr...  55 us
    dot_general x1, matrix products, body(): jnp.dot(normal_tile, lax.all_gather(directions, 'col', axis=0, tiled=True...  38.8 us
    reduce_scatter x1, waiting for transfers between devices, body(): lax.psum_scatter(partial_sum, 'row', scatter_dimension=0, tiled=True)  31.3 us
    unnamed x15, local copies, waits for them, and re-layouts  18.4 us
    dynamic_update_slice x1, other arithmetic, body(): lax.dynamic_update_slice_in_dim(normal_tile, current + terr_added, row_in...  13.6 us
    all_gather x1, waiting for transfers between devices, body(): lax.all_gather(directions, 'col', axis=0, tiled=True)  12.9 us
  transfers between devices with their start and end apart: 7, of which 6 were waited for; matrix products, arithmetic and copies ran while one was open for 21% of the time, Pallas kernels for 0%

profile of v1, /device:TPU:0, one launch (start us, length us, event | category | flops | bytes accessed | tf_op | source)
XLA Modules:
  0.0 574.9 jit_solution(2515322825823113102)
XLA Ops:
  7.2 0.0 all-gather.6.cloned.1.call-start
  7.2 0.7 all-gather.6.cloned.1.call-update
  7.9 0.0 all-gather.4.cloned.1.call-start
  8.0 11.8 %fusion.9 = bf16[576,2048]{1,0:T(8,128)(2,1)} fusion(bf16[576,2048]{1,0:T(8,128)(2,1)} %param.6, bf16[2048,2048]{1,0:T(8,128)(2,1)} %param.7, s32[2048]{0:T(1024)} %param.8), kind=kOutput, calls=%fused_computation.12 | convolution fusion | flops 4852154368 | bytes 13115392 | tf_op jit(solution)/shard_map/dot_general | solution.py:13
  19.8 0.0 all-gather.8.cloned.1.call-start
  19.8 0.5 collective-permute-start
  20.4 28.7 %collective-permute-done = bf16[576,2048]{1,0:T(8,128)(2,1)S(1)} collective-permute-done((bf16[576,2048]{1,0:T(8,128)(2,1)}, bf16[576,2048]{1,0:T(8,128)(2,1)S(1)}, u32[]{:S(2)}, u32[]{:S(2)}) %collective-permute-start) | collective-permute-done | bytes 2359328 | tf_op jit(solution)/shard_map/ppermute | solution.py:28
  49.0 0.0 collective-permute-start.1
  49.1 0.0 reduce-scatter.2.cloned.1.call-start
  49.2 28.3 %collective-permute-done.1 = bf16[576,2048]{1,0:T(8,128)(2,1)} collective-permute-done((bf16[576,2048]{1,0:T(8,128)(2,1)S(1)}, bf16[576,2048]{1,0:T(8,128)(2,1)}, u32[]{:S(2)}, u32[]{:S(2)}) %collective-permute-start.1) | collective-permute-done | bytes 2359328 | tf_op jit(solution)/shard_map/ppermute | solution.py:28
  77.5 0.1 fusion.17
  77.7 1.9 copy.12
  79.6 1.8 broadcast_select_fusion
  81.5 3.5 copy.14
  85.0 3.4 fusion.13
  88.3 0.5 copy.15
  88.8 6.8 %broadcast_multiply_fusion = f32[576,36,128]{2,1,0:T(8,128)} fusion(f32[576,128]{1,0:T(8,128)S(1)} %constant_dynamic-slice_fusion, f32[576,36]{1,0:T(8,128)S(1)} %fusion.17), kind=kLoop, calls=%fused_computation.10 | loop fusion | flops 2654208 | bytes 10994688 | tf_op jit(solution)/shard_map/mul | solution.py:54
  95.6 10.4 %collective-permute-done.2 = bf16[576,2048]{1,0:T(8,128)(2,1)} collective-permute-done((bf16[576,2048]{1,0:T(8,128)(2,1)}, bf16[576,2048]{1,0:T(8,128)(2,1)}, u32[]{:S(2)}, u32[]{:S(2)}) %collective-permute-start.2) | collective-permute-done | bytes 2359328 | tf_op jit(solution)/shard_map/ppermute | solution.py:28
  106.0 3.4 constant_dynamic-update-slice_fusion.7
  109.4 3.4 constant_dynamic-update-slice_fusion.6
  112.8 1.6 constant_dynamic-update-slice_fusion.5
  114.4 1.5 constant_dynamic-update-slice_fusion.4
  116.0 3.5 constant_dynamic-update-slice_fusion.3
  119.4 3.4 constant_dynamic-update-slice_fusion.2
  122.8 1.6 constant_dynamic-update-slice_fusion.1
  124.4 1.6 constant_dynamic-update-slice_fusion
  126.0 290.7 %all-gather.4.cloned.1.call-done = bf16[4608,2048]{1,0:T(8,128)(2,1)} async-done(((bf16[576,2048]{1,0:T(8,128)(2,1)}), bf16[4608,2048]{1,0:T(8,128)(2,1)}) %all-gather.4.cloned.1.call-update) | async-done | bytes 18874384 | tf_op jit(solution)/shard_map/all_gather | solution.py:23
  416.7 55.0 %fusion.3 = f32[2304,4608]{1,0:T(8,128)} fusion(bf16[4608,2048]{1,0:T(8,128)(2,1)} %all-gather.4.cloned.1.call-done, bf16[4608,2048]{1,0:T(8,128)(2,1)} %constant_dynamic-update-slice_fusion, s32[]{:T(128)S(6)} %select_n.43), kind=kOutput, calls=%fused_computation.5 | convolution fusion | flops 43486543872 | bytes 70778880 | tf_op jit(solution)/shard_map/dot_general | solution.py:32
  471.7 13.6 %fusion.2 = f32[2304,4608]{1,0:T(8,128)} fusion(f32[2304,4608]{1,0:T(8,128)} %fusion.3, s32[]{:T(128)S(6)} %select_n.44, f32[72,8,36,128]{3,2,1,0:T(8,128)} %bitcast.27), kind=kLoop, calls=%fused_computation.4 | loop fusion | flops 2654208 | bytes 33030148 | tf_op jit(solution)/shard_map/dynamic_update_slice | solution.py:56
  485.3 12.9 %all-gather.8.cloned.1.call-done = f32[4608,256]{1,0:T(8,128)} async-done(((f32[576,256]{1,0:T(8,128)}), f32[4608,256]{1,0:T(8,128)}) %all-gather.8.cloned.1.call-update) | async-done | bytes 4718608 | tf_op jit(solution)/shard_map/all_gather | solution.py:62
  498.2 38.8 %fusion.27 = f32[2304,256]{1,0:T(8,128)} fusion(f32[2304,4608]{1,0:T(8,128)} %fusion.2, f32[4608,256]{1,0:T(8,128)} %all-gather.8.cloned.1.call-done), kind=kOutput, calls=%fused_computation.50 | convolution fusion | flops 32614907904 | bytes 49545216 | tf_op jit(solution)/shard_map/dot_general | solution.py:60
  537.0 31.3 %reduce-scatter.2.cloned.1.call-done = f32[576,256]{1,0:T(8,128)} async-done(((f32[2304,256]{1,0:T(8,128)}), f32[576,256]{1,0:T(8,128)}) %reduce-scatter.2.cloned.1.call-update) | async-done | bytes 589840 | tf_op jit(solution)/shard_map/reduce_scatter | solution.py:66
  (19 shorter events, 0.2 us)
Async XLA Ops:
  7.2 70.5 %all-gather.6.cloned.1.call-start = ((), (), s32[]{:S(2)}) async-start(), calls=%async_computation.2 | async-start | bytes 1327104 | tf_op jit(solution)/shard_map/all_gather | solution.py:24
  7.9 69.6 %copy-start.3 = (s32[36]{0:T(128)S(1)}, s32[36]{0:T(128)}, u32[]{:S(2)}) copy-start(s32[36]{0:T(128)} %param.10) | copy-start | bytes 436
  7.9 408.8 %all-gather.4.cloned.1.call-start = ((), (), s32[]{:S(2)}) async-start(), calls=%async_computation.1 | async-start | bytes 21233664 | tf_op jit(solution)/shard_map/all_gather | solution.py:23
  19.8 478.4 %all-gather.8.cloned.1.call-start = ((), (), s32[]{:S(2)}) async-start(), calls=%async_computation.3 | async-start | bytes 5308416 | tf_op jit(solution)/shard_map/all_gather | solution.py:62
  19.8 29.2 %collective-permute-start = (bf16[576,2048]{1,0:T(8,128)(2,1)}, bf16[576,2048]{1,0:T(8,128)(2,1)S(1)}, u32[]{:S(2)}, u32[]{:S(2)}) collective-permute-start(bf16[576,2048]{1,0:T(8,128)(2,1)} %fusion.9), channel_id=1, source_target_pairs={{0,8},{8,16},{16,24},{24,0},{1,9},{9,17},{17,25},{25,1},{2,10},{10... | collective-permute-start | bytes 7077896 | tf_op jit(solution)/shard_map/ppermute | solution.py:28
  49.0 28.6 %copy-start.1 = (bf16[576,2048]{1,0:T(8,128)(2,1)}, bf16[576,2048]{1,0:T(8,128)(2,1)S(1)}, u32[]{:S(2)}) copy-start(bf16[576,2048]{1,0:T(8,128)(2,1)S(1)} %collective-permute-done) | copy-start | bytes 7077892
  49.0 28.4 %collective-permute-start.1 = (bf16[576,2048]{1,0:T(8,128)(2,1)S(1)}, bf16[576,2048]{1,0:T(8,128)(2,1)}, u32[]{:S(2)}, u32[]{:S(2)}) collective-permute-start(bf16[576,2048]{1,0:T(8,128)(2,1)S(1)} %collective-permute-done), channel_id=1, source_target_pairs={{0,8},{8,16},{16,24},{24,0},{1,9},{9,17},{17,25},{25,1},{2,10},{10... | collective-permute-start | bytes 7077896 | tf_op jit(solution)/shard_map/ppermute | solution.py:28
  49.1 519.2 %reduce-scatter.2.cloned.1.call-start = ((), (), s32[]{:S(2)}) async-start(), calls=%async_computation.4 | async-start | bytes 2949120 | tf_op jit(solution)/shard_map/reduce_scatter | solution.py:66
  77.4 28.6 %collective-permute-start.2 = (bf16[576,2048]{1,0:T(8,128)(2,1)}, bf16[576,2048]{1,0:T(8,128)(2,1)}, u32[]{:S(2)}, u32[]{:S(2)}) collective-permute-start(bf16[576,2048]{1,0:T(8,128)(2,1)} %collective-permute-done.1), channel_id=1, source_target_pairs={{0,8},{8,16},{16,24},{24,0},{1,9},{9,17},{17,25},{25,1},{2,10},{10... | collective-permute-start | bytes 7077896 | tf_op jit(solution)/shard_map/ppermute | solution.py:28
  88.8 24.0 %copy-start.2 = (bf16[576,2048]{1,0:T(8,128)(2,1)S(1)}, bf16[576,2048]{1,0:T(8,128)(2,1)}, u32[]{:S(2)}) copy-start(bf16[576,2048]{1,0:T(8,128)(2,1)} %copy-done.1) | copy-start | bytes 7077892
  95.6 18.8 %copy-start = (bf16[576,2048]{1,0:T(8,128)(2,1)S(1)}, bf16[576,2048]{1,0:T(8,128)(2,1)}, u32[]{:S(2)}) copy-start(bf16[576,2048]{1,0:T(8,128)(2,1)} %fusion.9) | copy-start | bytes 7077892
Sparse Core Ops, SparseCore 0:
  10.2 43.8 all-gather.5
  55.6 361.0 all-gather.3
  418.9 79.2 all-gather.7
  537.2 31.1 reduce-scatter.1
